TPU v7x, 256 devices: a whole 4x4x8 slice. The times are simulated.
256 devices in a mesh: rows: 256 (over z, x, y, core).
Axes of the slice: x: 4, y: 4, z: 8, core: 2. Of those that a mesh axis runs over, the one named last changes fastest.
Arguments:
- matrix: float32 [1048576, 128], P('rows')
- flips: int32 [1048576], P('rows'), may hold values from 0 to 1
- picks: int32 [16384], P('rows'), may hold values from 0 to 4095, as said below
Outputs:
- sketch: float32 [16384, 128], P('rows')
- factor: float32 [128, 128], replicated
Inputs may be any that keep to these rules, and one draw needn't show every extreme that they name: `picks`: each index lies within its owner's slab; repeated indices may occur.
All inputs are finite; a program needn't handle non-finite values.
Results may differ from a plain program's by a relative error of at most 0.00014.
Values sent between devices are 32-bit elements; how exact they have to be, the bound alone decides.
A program may use at most 64 MiB of HBM per device.

v0:
```python
import math
import jax
import jax.numpy as jnp
from jax import lax
from jax.sharding import PartitionSpec as P


def swapped(value, axis, stride):
    mask = 2**stride
    pairs = [(source, source ^ mask) for source in range(lax.axis_size(axis))]
    return lax.ppermute(value, axis, pairs)


def hadamard(order):
    index = lax.iota(jnp.int32, order)
    parity_sum = jnp.zeros((order, order), jnp.int32)
    for digit in range(order.bit_length()):
        parity_sum = parity_sum + (index[:, None] >> digit & 1) * (index[None, :] >> digit & 1)
    return (1 - 2 * (parity_sum % 2)).astype(jnp.float32)


def slab_transform(values):
    height = values.shape[0]
    width = values.shape[1]
    inner = 128
    outer = height // inner
    blocks = values.reshape(outer, inner, width)
    mixed = jnp.einsum(
        "ij,ajc->aic",
        hadamard(inner),
        blocks,
        precision=lax.Precision.HIGHEST,
        preferred_element_type=jnp.float32,
    )
    mixed = jnp.einsum(
        "ab,bic->aic",
        hadamard(outer),
        mixed,
        precision=lax.Precision.HIGHEST,
        preferred_element_type=jnp.float32,
    )
    return mixed.reshape(height, width)


def shards(matrix, flips, picks):
    devices = lax.axis_size("rows")
    digits = devices.bit_length() - 1
    myself = lax.axis_index("rows")
    height = matrix.shape[0]
    per_device = picks.shape[0]
    signs = (1 - 2 * flips).astype(jnp.float32)
    local = slab_transform(matrix * signs[:, None])
    scale = 1.0 / math.sqrt(height * devices)
    order_list = list(range(digits))
    values = local
    for digit in order_list:
        partner = swapped(values, "rows", digit)
        upper = myself >> digit & 1 == 1
        values = jnp.where(upper, partner - values, values + partner)
    sketch = jnp.take(values, picks, axis=0) * scale
    partial_gram = jnp.dot(
        sketch.T, sketch, preferred_element_type=jnp.float32, precision=lax.Precision.HIGHEST
    )
    gram = lax.psum(partial_gram, "rows") / (per_device * devices)
    factor = jnp.linalg.cholesky(gram)
    return (sketch, factor)


def solution(mesh):
    placed = (P("rows", None), P("rows"), P("rows"))
    return jax.shard_map(
        shards, mesh=mesh, in_specs=placed, out_specs=(P("rows", None), P()), check_vma=False
    )
```

profile of v0, /device:TPU:1, one launch (start us, length us, event | category | flops | bytes accessed | tf_op | source)
XLA Modules:
  0.0 735.6 jit_solution(15239661016108178442)
XLA Ops:
  8.0 2.2 broadcast_multiply_fusion
  10.2 5.0 fusion.7
  15.2 2.4 copy.10
  17.6 1.9 fusion
  19.5 1.2 copy.7
  20.7 3.3 collective-permute-start
  24.0 3.9 collective-permute-done
  28.0 2.4 add_select_fusion.7
  30.5 1.2 copy-done.1
  31.7 45.7 %collective-permute-done.1 = f32[4096,128]{1,0:T(8,128)} collective-permute-done((f32[4096,128]{1,0:T(8,128)S(1)}, f32[4096,128]{1,0:T(8,128)}, u32[]{:S(2)}, u32[]{:S(2)}) %collective-permute-start.1) | collective-permute-done | bytes 2097184 | tf_op jit(solution)/shard_map/ppermute | solution.py:11
  77.4 2.4 add_select_fusion.6
  79.9 1.3 collective-permute-start.2
  81.2 46.4 %collective-permute-done.2 = f32[4096,128]{1,0:T(8,128)} collective-permute-done((f32[4096,128]{1,0:T(8,128)S(1)}, f32[4096,128]{1,0:T(8,128)}, u32[]{:S(2)}, u32[]{:S(2)}) %collective-permute-start.2) | collective-permute-done | bytes 2097184 | tf_op jit(solution)/shard_map/ppermute | solution.py:11
  127.5 3.1 add_select_fusion.5
  130.7 45.4 %collective-permute-done.3 = f32[4096,128]{1,0:T(8,128)} collective-permute-done((f32[4096,128]{1,0:T(8,128)}, f32[4096,128]{1,0:T(8,128)}, u32[]{:S(2)}, u32[]{:S(2)}) %collective-permute-start.3) | collective-permute-done | bytes 2097184 | tf_op jit(solution)/shard_map/ppermute | solution.py:11
  176.1 2.4 add_select_fusion.4
  178.5 1.1 collective-permute-start.4
  179.7 44.8 %collective-permute-done.4 = f32[4096,128]{1,0:T(8,128)} collective-permute-done((f32[4096,128]{1,0:T(8,128)S(1)}, f32[4096,128]{1,0:T(8,128)}, u32[]{:S(2)}, u32[]{:S(2)}) %collective-permute-start.4) | collective-permute-done | bytes 2097184 | tf_op jit(solution)/shard_map/ppermute | solution.py:11
  224.5 3.1 add_select_fusion.3
  227.6 43.7 %collective-permute-done.5 = f32[4096,128]{1,0:T(8,128)} collective-permute-done((f32[4096,128]{1,0:T(8,128)}, f32[4096,128]{1,0:T(8,128)}, u32[]{:S(2)}, u32[]{:S(2)}) %collective-permute-start.5) | collective-permute-done | bytes 2097184 | tf_op jit(solution)/shard_map/ppermute | solution.py:11
  271.3 2.4 add_select_fusion.2
  273.8 1.7 collective-permute-start.6
  275.5 91.6 %collective-permute-done.6 = f32[4096,128]{1,0:T(8,128)} collective-permute-done((f32[4096,128]{1,0:T(8,128)S(1)}, f32[4096,128]{1,0:T(8,128)}, u32[]{:S(2)}, u32[]{:S(2)}) %collective-permute-start.6) | collective-permute-done | bytes 2097184 | tf_op jit(solution)/shard_map/ppermute | solution.py:11
  367.1 2.4 add_select_fusion.1
  369.5 5.1 collective-permute-start.7
  374.7 90.6 %collective-permute-done.7 = f32[4096,128]{1,0:T(8,128)} collective-permute-done((f32[4096,128]{1,0:T(8,128)S(1)}, f32[4096,128]{1,0:T(8,128)}, u32[]{:S(2)}, u32[]{:S(2)}) %collective-permute-start.7) | collective-permute-done | bytes 2097184 | tf_op jit(solution)/shard_map/ppermute | solution.py:11
  465.3 3.1 add_select_fusion
  468.4 2.2 gather_fusion
  470.7 0.9 fusion.62
  471.7 241.6 %all-reduce.2.cloned.1.call-done = f32[128,128]{0,1:T(8,128)} async-done(((f32[128,128]{0,1:T(8,128)}), f32[128,128]{0,1:T(8,128)}) %all-reduce.2.cloned.1.call-update) | async-done | bytes 65552 | tf_op jit(solution)/shard_map/psum | solution.py:64
  715.0 11.7 %cholesky.18 = f32[128,128]{1,0:T(8,128)S(1)} custom-call(f32[128,128]{1,0:T(8,128)S(1)} %fusion.9), custom_call_target="Cholesky" | custom-call | tf_op jit(solution)/shard_map/jit(cholesky)/cholesky | solution.py:65
  727.4 1.3 select_select_fusion
  (31 shorter events, 3.5 us)
Async XLA Ops:
  7.2 706.1 %all-reduce.2.cloned.1.call-start = ((), (), s32[]{:S(2)}) async-start(), calls=%async_computation | async-start | bytes 131072 | tf_op jit(solution)/shard_map/psum | solution.py:64
  20.7 3.3 copy-start.2
  20.7 7.2 collective-permute-start
  30.4 1.3 copy-start.1
  30.4 47.0 %collective-permute-start.1 = (f32[4096,128]{1,0:T(8,128)S(1)}, f32[4096,128]{1,0:T(8,128)}, u32[]{:S(2)}, u32[]{:S(2)}) collective-permute-start(f32[4096,128]{1,0:T(8,128)S(1)} %add_select_fusion.7), channel_id=1, source_target_pairs={{0,2},{1,3},{2,0},{3,1},{4,6},{5,7},{6,4},{7,5},{8,10},{9,11},{10,... | collective-permute-start | bytes 6291464 | tf_op jit(solution)/shard_map/ppermute | solution.py:11
  79.9 47.7 %collective-permute-start.2 = (f32[4096,128]{1,0:T(8,128)S(1)}, f32[4096,128]{1,0:T(8,128)}, u32[]{:S(2)}, u32[]{:S(2)}) collective-permute-start(f32[4096,128]{1,0:T(8,128)S(1)} %add_select_fusion.6), channel_id=1, source_target_pairs={{0,4},{1,5},{2,6},{3,7},{4,0},{5,1},{6,2},{7,3},{8,12},{9,13},{10,... | collective-permute-start | bytes 6291464 | tf_op jit(solution)/shard_map/ppermute | solution.py:11
  130.7 45.4 %collective-permute-start.3 = (f32[4096,128]{1,0:T(8,128)}, f32[4096,128]{1,0:T(8,128)}, u32[]{:S(2)}, u32[]{:S(2)}) collective-permute-start(f32[4096,128]{1,0:T(8,128)} %add_select_fusion.5), channel_id=1, source_target_pairs={{0,8},{1,9},{2,10},{3,11},{4,12},{5,13},{6,14},{7,15},{8,0},{9,1},... | collective-permute-start | bytes 6291464 | tf_op jit(solution)/shard_map/ppermute | solution.py:11
  178.5 45.9 %collective-permute-start.4 = (f32[4096,128]{1,0:T(8,128)S(1)}, f32[4096,128]{1,0:T(8,128)}, u32[]{:S(2)}, u32[]{:S(2)}) collective-permute-start(f32[4096,128]{1,0:T(8,128)S(1)} %add_select_fusion.4), channel_id=1, source_target_pairs={{0,16},{1,17},{2,18},{3,19},{4,20},{5,21},{6,22},{7,23},{8,24},{9,... | collective-permute-start | bytes 6291464 | tf_op jit(solution)/shard_map/ppermute | solution.py:11
  227.6 43.7 %collective-permute-start.5 = (f32[4096,128]{1,0:T(8,128)}, f32[4096,128]{1,0:T(8,128)}, u32[]{:S(2)}, u32[]{:S(2)}) collective-permute-start(f32[4096,128]{1,0:T(8,128)} %add_select_fusion.3), channel_id=1, source_target_pairs={{0,32},{1,33},{2,34},{3,35},{4,36},{5,37},{6,38},{7,39},{8,40},{9,... | collective-permute-start | bytes 6291464 | tf_op jit(solution)/shard_map/ppermute | solution.py:11
  273.8 1.7 copy-start
  273.8 93.3 %collective-permute-start.6 = (f32[4096,128]{1,0:T(8,128)S(1)}, f32[4096,128]{1,0:T(8,128)}, u32[]{:S(2)}, u32[]{:S(2)}) collective-permute-start(f32[4096,128]{1,0:T(8,128)S(1)} %add_select_fusion.2), channel_id=1, source_target_pairs={{0,64},{1,65},{2,66},{3,67},{4,68},{5,69},{6,70},{7,71},{8,72},{9,... | collective-permute-start | bytes 6291464 | tf_op jit(solution)/shard_map/ppermute | solution.py:11
  275.5 99.2 %copy-start.4 = (s32[64]{0:T(128)S(1)}, s32[64]{0:T(128)}, u32[]{:S(2)}) copy-start(s32[64]{0:T(128)} %param.5) | copy-start | bytes 772
  369.5 95.8 %collective-permute-start.7 = (f32[4096,128]{1,0:T(8,128)S(1)}, f32[4096,128]{1,0:T(8,128)}, u32[]{:S(2)}, u32[]{:S(2)}) collective-permute-start(f32[4096,128]{1,0:T(8,128)S(1)} %add_select_fusion.1), channel_id=1, source_target_pairs={{0,128},{1,129},{2,130},{3,131},{4,132},{5,133},{6,134},{7,135},{8... | collective-permute-start | bytes 6291464 | tf_op jit(solution)/shard_map/ppermute | solution.py:11
  470.7 258.0 %copy-start.3 = (f32[64,128]{1,0:T(8,128)}, f32[64,128]{1,0:T(8,128)S(1)}, u32[]{:S(2)}) copy-start(f32[64,128]{1,0:T(8,128)S(1)} %select_multiply_fusion) | copy-start | bytes 98308
Sparse Core Ops, SparseCore 0:
  471.8 241.3 all-reduce.1
where the time goes:
time: 736 us
  waiting for transfers between devices  654 us (89%)
  other arithmetic  40.1 us (5%)
  between operations  14.2 us (2%)
  starting transfers between devices  12.7 us (2%)
  matrix products  7.84 us (1%)
    ppermute x8, waiting for transfers between devices, swapped(): return lax.ppermute(value, axis, pairs)  412 us
    psum x1, waiting for transfers between devices, shards(): gram = lax.psum(partial_gram, 'rows') / (per_device * devices)  242 us
    select_n x8, other arithmetic, shards(): values = jnp.where(upper, partner - values, values + partner)  21.6 us
  transfers between devices with their start and end apart: 9, of which 9 were waited for; matrix products, arithmetic and copies ran while one was open for 0% of the time, Pallas kernels for 0%

commit v1 on v0

--- a/solution.py
+++ b/solution.py
@@ -61,7 +61,7 @@
     partial_gram = jnp.dot(
         sketch.T, sketch, preferred_element_type=jnp.float32, precision=lax.Precision.HIGHEST
     )
-    gram = lax.psum(partial_gram, "rows") / (per_device * devices)
+    gram = lax.all_gather(partial_gram, axis_name="rows").sum(axis=0) / (per_device * devices)
     factor = jnp.linalg.cholesky(gram)
     return (sketch, factor)
 

time: 736 us -> 625 us (0.85)
  waiting for transfers between devices: 654 us -> 538 us
    psum x1 -> x0, waiting for transfers between devices: 242 us -> none  [shards(): gram = lax.psum(partial_gram, 'rows') / (per_device * devices)]
    all_gather x0 -> x1, waiting for transfers between devices: none -> 125 us  [shards(): lax.all_gather(partial_gram, axis_name='rows').sum(axis=0)]
where the time goes in v1:
time: 625 us; the launch traced here: 624 us
  waiting for transfers between devices  538 us (86%)
  other arithmetic  45 us (7%)
  between operations  14.2 us (2%)
  starting transfers between devices  12.7 us (2%)
  matrix products  7.83 us (1%)
  local copies, waits for them, and re-layouts  7.11 us (1%)
    ppermute x8, waiting for transfers between devices, swapped(): return lax.ppermute(value, axis, pairs)  412 us
    all_gather x1, waiting for transfers between devices, shards(): lax.all_gather(partial_gram, axis_name='rows').sum(axis=0)  125 us
    select_n x8, other arithmetic, shards(): values = jnp.where(upper, partner - values, values + partner)  21.6 us
    ppermute x8, starting transfers between devices, swapped(): return lax.ppermute(value, axis, pairs)  12.6 us
  transfers between devices with their start and end apart: 9, of which 9 were waited for; matrix products, arithmetic and copies ran while one was open for 0% of the time, Pallas kernels for 0%

profile of v1, /device:TPU:1, one launch (start us, length us, event | category | flops | bytes accessed | tf_op | source)
XLA Modules:
  0.0 624.4 jit_solution(3989698631527770779)
XLA Ops:
  8.0 2.2 broadcast_multiply_fusion
  10.2 5.0 convolution_bitcast_fusion
  15.2 2.4 copy.9
  17.6 1.9 fusion.34
  19.5 1.2 copy.10
  20.7 3.3 collective-permute-start
  24.0 3.9 collective-permute-done
  28.0 2.4 add_select_fusion.7
  30.5 1.2 copy-done.1
  31.7 45.7 %collective-permute-done.1 = f32[4096,128]{1,0:T(8,128)} collective-permute-done((f32[4096,128]{1,0:T(8,128)S(1)}, f32[4096,128]{1,0:T(8,128)}, u32[]{:S(2)}, u32[]{:S(2)}) %collective-permute-start.1) | collective-permute-done | bytes 2097184 | tf_op jit(solution)/shard_map/ppermute | solution.py:11
  77.4 2.4 add_select_fusion.6
  79.9 1.3 collective-permute-start.2
  81.2 46.4 %collective-permute-done.2 = f32[4096,128]{1,0:T(8,128)} collective-permute-done((f32[4096,128]{1,0:T(8,128)S(1)}, f32[4096,128]{1,0:T(8,128)}, u32[]{:S(2)}, u32[]{:S(2)}) %collective-permute-start.2) | collective-permute-done | bytes 2097184 | tf_op jit(solution)/shard_map/ppermute | solution.py:11
  127.5 3.1 add_select_fusion.5
  130.7 45.4 %collective-permute-done.3 = f32[4096,128]{1,0:T(8,128)} collective-permute-done((f32[4096,128]{1,0:T(8,128)}, f32[4096,128]{1,0:T(8,128)}, u32[]{:S(2)}, u32[]{:S(2)}) %collective-permute-start.3) | collective-permute-done | bytes 2097184 | tf_op jit(solution)/shard_map/ppermute | solution.py:11
  176.1 2.4 add_select_fusion.4
  178.5 1.1 collective-permute-start.4
  179.7 44.8 %collective-permute-done.4 = f32[4096,128]{1,0:T(8,128)} collective-permute-done((f32[4096,128]{1,0:T(8,128)S(1)}, f32[4096,128]{1,0:T(8,128)}, u32[]{:S(2)}, u32[]{:S(2)}) %collective-permute-start.4) | collective-permute-done | bytes 2097184 | tf_op jit(solution)/shard_map/ppermute | solution.py:11
  224.5 3.1 add_select_fusion.3
  227.6 43.7 %collective-permute-done.5 = f32[4096,128]{1,0:T(8,128)} collective-permute-done((f32[4096,128]{1,0:T(8,128)}, f32[4096,128]{1,0:T(8,128)}, u32[]{:S(2)}, u32[]{:S(2)}) %collective-permute-start.5) | collective-permute-done | bytes 2097184 | tf_op jit(solution)/shard_map/ppermute | solution.py:11
  271.3 2.4 add_select_fusion.2
  273.8 1.7 collective-permute-start.6
  275.5 91.6 %collective-permute-done.6 = f32[4096,128]{1,0:T(8,128)} collective-permute-done((f32[4096,128]{1,0:T(8,128)S(1)}, f32[4096,128]{1,0:T(8,128)}, u32[]{:S(2)}, u32[]{:S(2)}) %collective-permute-start.6) | collective-permute-done | bytes 2097184 | tf_op jit(solution)/shard_map/ppermute | solution.py:11
  367.1 2.4 add_select_fusion.1
  369.5 5.1 collective-permute-start.7
  374.7 90.6 %collective-permute-done.7 = f32[4096,128]{1,0:T(8,128)} collective-permute-done((f32[4096,128]{1,0:T(8,128)S(1)}, f32[4096,128]{1,0:T(8,128)}, u32[]{:S(2)}, u32[]{:S(2)}) %collective-permute-start.7) | collective-permute-done | bytes 2097184 | tf_op jit(solution)/shard_map/ppermute | solution.py:11
  465.3 3.1 add_select_fusion
  468.4 2.2 gather_fusion
  471.7 125.5 %all-gather.3.cloned.1.call-done = f32[32768,128]{1,0:T(8,128)} async-done(((f32[128,128]{1,0:T(8,128)}), f32[32768,128]{1,0:T(8,128)}) %all-gather.3.cloned.1.call-update) | async-done | bytes 16777232 | tf_op jit(solution)/shard_map/all_gather | solution.py:64
  597.1 6.6 %reduce_sum.11 = f32[128,128]{1,0:T(8,128)S(1)} reduce(f32[256,128,128]{2,1,0:T(8,128)} %bitcast.20, f32[]{:T(128)} %constant.127.clone.1), dimensions={0}, to_apply=%region_0.1 | reduce | flops 4177920 | bytes 16842756 | tf_op jit(solution)/shard_map/reduce_sum | solution.py:64
  603.8 11.7 %cholesky.18 = f32[128,128]{1,0:T(8,128)S(1)} custom-call(f32[128,128]{1,0:T(8,128)S(1)} %fusion.6), custom_call_target="Cholesky" | custom-call | tf_op jit(solution)/shard_map/jit(cholesky)/cholesky | solution.py:65
  616.3 1.3 select_select_fusion
  (31 shorter events, 2.8 us)
Async XLA Ops:
  7.2 590.0 %all-gather.3.cloned.1.call-start = ((), (), s32[]{:S(2)}) async-start(), calls=%async_computation | async-start | bytes 16842752 | tf_op jit(solution)/shard_map/all_gather | solution.py:64
  20.7 3.3 copy-start.2
  20.7 7.2 %collective-permute-start = (f32[4096,128]{1,0:T(8,128)S(1)}, f32[4096,128]{1,0:T(8,128)}, u32[]{:S(2)}, u32[]{:S(2)}) collective-permute-start(f32[4096,128]{1,0:T(8,128)S(1)} %bitcast.21), channel_id=1, source_target_pairs={{0,1},{1,0},{2,3},{3,2},{4,5},{5,4},{6,7},{7,6},{8,9},{9,8},{10,11... | collective-permute-start | bytes 6291464 | tf_op jit(solution)/shard_map/ppermute | solution.py:11
  30.4 1.3 copy-start.1
  30.4 47.0 %collective-permute-start.1 = (f32[4096,128]{1,0:T(8,128)S(1)}, f32[4096,128]{1,0:T(8,128)}, u32[]{:S(2)}, u32[]{:S(2)}) collective-permute-start(f32[4096,128]{1,0:T(8,128)S(1)} %add_select_fusion.7), channel_id=1, source_target_pairs={{0,2},{1,3},{2,0},{3,1},{4,6},{5,7},{6,4},{7,5},{8,10},{9,11},{10,... | collective-permute-start | bytes 6291464 | tf_op jit(solution)/shard_map/ppermute | solution.py:11
  79.9 47.7 %collective-permute-start.2 = (f32[4096,128]{1,0:T(8,128)S(1)}, f32[4096,128]{1,0:T(8,128)}, u32[]{:S(2)}, u32[]{:S(2)}) collective-permute-start(f32[4096,128]{1,0:T(8,128)S(1)} %add_select_fusion.6), channel_id=1, source_target_pairs={{0,4},{1,5},{2,6},{3,7},{4,0},{5,1},{6,2},{7,3},{8,12},{9,13},{10,... | collective-permute-start | bytes 6291464 | tf_op jit(solution)/shard_map/ppermute | solution.py:11
  130.7 45.4 %collective-permute-start.3 = (f32[4096,128]{1,0:T(8,128)}, f32[4096,128]{1,0:T(8,128)}, u32[]{:S(2)}, u32[]{:S(2)}) collective-permute-start(f32[4096,128]{1,0:T(8,128)} %add_select_fusion.5), channel_id=1, source_target_pairs={{0,8},{1,9},{2,10},{3,11},{4,12},{5,13},{6,14},{7,15},{8,0},{9,1},... | collective-permute-start | bytes 6291464 | tf_op jit(solution)/shard_map/ppermute | solution.py:11
  178.5 45.9 %collective-permute-start.4 = (f32[4096,128]{1,0:T(8,128)S(1)}, f32[4096,128]{1,0:T(8,128)}, u32[]{:S(2)}, u32[]{:S(2)}) collective-permute-start(f32[4096,128]{1,0:T(8,128)S(1)} %add_select_fusion.4), channel_id=1, source_target_pairs={{0,16},{1,17},{2,18},{3,19},{4,20},{5,21},{6,22},{7,23},{8,24},{9,... | collective-permute-start | bytes 6291464 | tf_op jit(solution)/shard_map/ppermute | solution.py:11
  227.6 43.7 %collective-permute-start.5 = (f32[4096,128]{1,0:T(8,128)}, f32[4096,128]{1,0:T(8,128)}, u32[]{:S(2)}, u32[]{:S(2)}) collective-permute-start(f32[4096,128]{1,0:T(8,128)} %add_select_fusion.3), channel_id=1, source_target_pairs={{0,32},{1,33},{2,34},{3,35},{4,36},{5,37},{6,38},{7,39},{8,40},{9,... | collective-permute-start | bytes 6291464 | tf_op jit(solution)/shard_map/ppermute | solution.py:11
  273.8 1.7 copy-start
  273.8 93.3 %collective-permute-start.6 = (f32[4096,128]{1,0:T(8,128)S(1)}, f32[4096,128]{1,0:T(8,128)}, u32[]{:S(2)}, u32[]{:S(2)}) collective-permute-start(f32[4096,128]{1,0:T(8,128)S(1)} %add_select_fusion.2), channel_id=1, source_target_pairs={{0,64},{1,65},{2,66},{3,67},{4,68},{5,69},{6,70},{7,71},{8,72},{9,... | collective-permute-start | bytes 6291464 | tf_op jit(solution)/shard_map/ppermute | solution.py:11
  275.5 99.2 %copy-start.4 = (s32[64]{0:T(128)S(1)}, s32[64]{0:T(128)}, u32[]{:S(2)}) copy-start(s32[64]{0:T(128)} %param.5) | copy-start | bytes 772
  369.5 95.8 %collective-permute-start.7 = (f32[4096,128]{1,0:T(8,128)S(1)}, f32[4096,128]{1,0:T(8,128)}, u32[]{:S(2)}, u32[]{:S(2)}) collective-permute-start(f32[4096,128]{1,0:T(8,128)S(1)} %add_select_fusion.1), channel_id=1, source_target_pairs={{0,128},{1,129},{2,130},{3,131},{4,132},{5,133},{6,134},{7,135},{8... | collective-permute-start | bytes 6291464 | tf_op jit(solution)/shard_map/ppermute | solution.py:11
  470.7 133.0 %copy-start.3 = (f32[64,128]{1,0:T(8,128)}, f32[64,128]{1,0:T(8,128)S(1)}, u32[]{:S(2)}) copy-start(f32[64,128]{1,0:T(8,128)S(1)} %select_multiply_fusion) | copy-start | bytes 98308
Sparse Core Ops, SparseCore 0:
  471.8 125.2 all-gather.2
